TPU v7x, 32 devices: a whole 2x2x4 slice. The times are simulated.
32 devices in a mesh: dp: 8 (over z, x), ctx: 4 (over y, core).
Axes of the slice: x: 2, y: 2, z: 4, core: 2. Of those that a mesh axis runs over, the one named last changes fastest.
Arguments:
- inputs: bfloat16 [8, 512, 5376], P('dp', 'ctx'), may hold values from -6 to 6
- q_proj: bfloat16 [8, 512, 2048], P('dp', 'ctx'), may hold values from -260 to 260
- k_proj: bfloat16 [8, 512, 1024], P('dp', 'ctx'), may hold values from -260 to 260
- v_proj: bfloat16 [8, 512, 1024], P('dp', 'ctx'), may hold values from -6 to 6
- d_attn: bfloat16 [8, 512, 2048], P('dp', 'ctx'), may hold values from -6 to 6
- positions: int32 [8, 512], P('dp', 'ctx'), may hold values from 0 to 511, as said below
- windows: int32 [8], P('dp'), may hold values from 512 to 1024
- q_gain: float32 [128], replicated, may hold values from 0.7 to 5.5
- k_gain: float32 [128], replicated, may hold values from 0.7 to 5.5
- weight: bfloat16 [5376, 4096], P('dp'), may hold values from -0.078125 to 0.078125
Outputs:
- d_inputs: bfloat16 [8, 512, 5376], P('dp', 'ctx')
- d_weight_t: float32 [4096, 5376], P('ctx', 'dp')
- d_q_gain: float32 [128], replicated
- d_k_gain: float32 [128], replicated
Inputs may be any that keep to these rules, and one draw needn't show every extreme that they name: `positions`: within each sequence a position counts the tokens since its document began: it grows by one from token to token and falls to 0 where a document begins; the first token of a sequence has position 0. Some sequence holds a single document.
All inputs are finite; a program needn't handle non-finite values.
Results may differ from a plain program's by a relative error of at most 0.029.
Values may be sent and summed in bfloat16 or wider, within the bound.
A program may use at most 128 MiB of HBM per device.

v0:
```python
import math
import jax
import jax.numpy as jnp
from jax import lax
from jax.sharding import PartitionSpec as P

REACH = 8
score_scale = 168.0 ** (-0.5)
rope_base = 10000.0
norm_eps = 1e-06


def from_behind(value, axis, steps):
    count = lax.axis_size(axis)
    initial, last = (max(0, -steps), min(count, count - steps))
    return lax.ppermute(value, axis, [(source, source + steps) for source in range(initial, last)])


def rotated_unit(projected_rows, gain_vector, token_pos, head_count):
    head_width = gain_vector.shape[0]
    rows_heads = projected_rows.reshape(projected_rows.shape[0], head_count, head_width)
    inverse = lax.rsqrt(jnp.mean(rows_heads * rows_heads, axis=-1, keepdims=True) + norm_eps)
    normed = rows_heads * inverse * gain_vector
    half_width = head_width // 2
    frequency = jnp.exp(
        jnp.arange(half_width, dtype=jnp.float32) * (-2.0 * math.log(rope_base) / head_width)
    )
    angles = token_pos.astype(jnp.float32)[:, None] * frequency[None, :]
    cosine_table = jnp.cos(angles)[:, None, :]
    sine_table = jnp.sin(angles)[:, None, :]
    first_half = normed[..., :half_width]
    second_half = normed[..., half_width:]
    return jnp.concatenate(
        [
            first_half * cosine_table - second_half * sine_table,
            second_half * cosine_table + first_half * sine_table,
        ],
        axis=-1,
    )


def shards(inputs, q_proj, k_proj, v_proj, d_attn, positions, windows, q_gain, k_gain, weight):
    tok_rows = inputs.shape[1]
    head_width = q_gain.shape[0]
    query_heads = q_proj.shape[2] // head_width
    key_heads = k_proj.shape[2] // head_width
    group_size = query_heads // key_heads
    token_pos = positions[0]
    window = windows[0]
    input_cols = lax.all_to_all(inputs, "dp", split_axis=2, concat_axis=0, tiled=True)

    def query_side(projected_rows, gain_vector):
        return rotated_unit(projected_rows, gain_vector, token_pos, query_heads)

    def key_side(projected_rows, gain_vector):
        return rotated_unit(projected_rows, gain_vector, token_pos, key_heads)

    q_full, query_back = jax.vjp(query_side, q_proj[0].astype(jnp.float32), q_gain)
    k_full, key_back = jax.vjp(key_side, k_proj[0].astype(jnp.float32), k_gain)
    query_rotated = q_full.astype(jnp.bfloat16).reshape(tok_rows, key_heads, group_size, head_width)
    key_rotated = k_full.astype(jnp.bfloat16)
    v_own = v_proj[0].reshape(tok_rows, key_heads, head_width)
    reach_count = min(REACH, lax.axis_size("ctx") - 1)
    key_blocks = [key_rotated]
    value_blocks = [v_own]
    for distance_steps in range(1, reach_count + 1):
        far_keys, far_values = from_behind((key_rotated, v_own), "ctx", distance_steps)
        key_blocks.append(far_keys)
        value_blocks.append(far_values)
    all_keys = jnp.stack(key_blocks)
    all_values = jnp.stack(value_blocks)
    block_ids = jnp.arange(reach_count + 1, dtype=jnp.int32)
    offsets = jnp.arange(tok_rows, dtype=jnp.int32)
    distance = block_ids[None, :, None] * tok_rows + offsets[:, None, None] - offsets[None, None, :]
    allowed = (distance >= 0) & (distance < window) & (distance <= token_pos[:, None, None])
    scores = (
        jnp.einsum("ahgd,bchd->hgabc", query_rotated, all_keys, preferred_element_type=jnp.float32)
        * score_scale
    )
    scores = jnp.where(allowed, scores, -jnp.inf)
    row_max = jnp.max(scores, axis=(3, 4), keepdims=True)
    exponent = jnp.exp(scores - row_max)
    probs = exponent / jnp.sum(exponent, axis=(3, 4), keepdims=True)
    head_gradient = d_attn[0].reshape(tok_rows, key_heads, group_size, head_width)
    dprobs = jnp.einsum(
        "ahgd,bchd->hgabc", head_gradient, all_values, preferred_element_type=jnp.float32
    )
    delta = jnp.sum(probs * dprobs, axis=(3, 4), keepdims=True)
    dscores = (probs * (dprobs - delta)).astype(jnp.bfloat16)
    probs_low = probs.astype(jnp.bfloat16)
    dq_rot = (
        jnp.einsum("hgabc,bchd->ahgd", dscores, all_keys, preferred_element_type=jnp.float32)
        * score_scale
    )
    dk_blocks = (
        jnp.einsum("hgabc,ahgd->bchd", dscores, query_rotated, preferred_element_type=jnp.float32)
        * score_scale
    )
    dv_blocks = jnp.einsum(
        "hgabc,ahgd->bchd", probs_low, head_gradient, preferred_element_type=jnp.float32
    )
    dk_total = dk_blocks[0]
    dv_total = dv_blocks[0]
    for distance_steps in range(1, reach_count + 1):
        back_keys, back_values = from_behind(
            (
                dk_blocks[distance_steps].astype(jnp.bfloat16),
                dv_blocks[distance_steps].astype(jnp.bfloat16),
            ),
            "ctx",
            -distance_steps,
        )
        dk_total = dk_total + back_keys.astype(jnp.float32)
        dv_total = dv_total + back_values.astype(jnp.float32)
    dq_proj, dq_gain = query_back(dq_rot.reshape(tok_rows, query_heads, head_width))
    dk_proj, dk_gain = key_back(dk_total)
    dq_gain_all, dk_gain_all = lax.psum((dq_gain, dk_gain), ("dp", "ctx"))
    dv_proj = dv_total.reshape(tok_rows, key_heads * head_width)
    d_proj = jnp.concatenate([dq_proj, dk_proj, dv_proj], axis=-1).astype(jnp.bfloat16)[None]
    gathered = lax.all_gather(d_proj, "dp", axis=0, tiled=True)
    d_cols = jnp.einsum("btp,dp->btd", gathered, weight, preferred_element_type=jnp.float32)
    d_inputs = lax.all_to_all(
        d_cols.astype(jnp.bfloat16), "dp", split_axis=0, concat_axis=2, tiled=True
    )
    d_weight_t = lax.psum_scatter(
        jnp.einsum("btp,btd->pd", gathered, input_cols, preferred_element_type=jnp.float32).astype(
            jnp.bfloat16
        ),
        "ctx",
        scatter_dimension=0,
        tiled=True,
    ).astype(jnp.float32)
    return (d_inputs, d_weight_t, dq_gain_all, dk_gain_all)


def solution(mesh):
    placed = (
        P("dp", "ctx", None),
        P("dp", "ctx", None),
        P("dp", "ctx", None),
        P("dp", "ctx", None),
        P("dp", "ctx", None),
        P("dp", "ctx"),
        P("dp"),
        P(),
        P(),
        P("dp", None),
    )
    return jax.shard_map(
        shards,
        mesh=mesh,
        in_specs=placed,
        out_specs=(P("dp", "ctx", None), P("ctx", "dp"), P(), P()),
        check_vma=False,
    )
```

profile of v0, /device:TPU:0, one launch (start us, length us, event | category | flops | bytes accessed | tf_op | source)
XLA Modules:
  0.0 321.0 jit_solution(8718791477971543858)
XLA Ops:
  11.7 5.0 %collective-permute-start.2 = (bf16[128,8,128]{2,0,1:T(8,128)(2,1)}, bf16[128,8,128]{2,0,1:T(8,128)(2,1)}, u32[]{:S(2)}, u32[]{:S(2)}) collective-permute-start(bf16[128,8,128]{2,0,1:T(8,128)(2,1)} %pad_maximum_fusion.3), channel_id=1, source_target_pairs={{0,3},{4,7},{8,11},{12,15},{16,19},{20,23},{24,27},{28,31}} | collective-permute-start | bytes 786440 | tf_op jit(solution)/shard_map/ppermute | solution.py:16
  16.7 2.0 collective-permute-start
  18.7 2.0 collective-permute-start.1
  21.7 2.0 collective-permute-start.3
  23.6 2.0 collective-permute-start.4
  32.9 2.1 fusion.7
  35.9 3.9 %collective-permute-done.5 = bf16[128,8,128]{2,0,1:T(8,128)(2,1)S(1)} collective-permute-done((bf16[128,8,128]{2,0,1:T(8,128)(2,1)}, bf16[128,8,128]{2,0,1:T(8,128)(2,1)S(1)}, u32[]{:S(2)}, u32[]{:S(2)}) %collective-permute-start.5) | collective-permute-done | bytes 262176 | tf_op jit(solution)/shard_map/ppermute | solution.py:16
  39.8 2.4 fusion.2
  45.2 2.2 fusion.57
  47.4 3.0 fusion.56
  58.1 1.8 multiply_add_fusion.1
  74.0 2.3 collective-permute-done.10
  76.3 6.4 %collective-permute-done.11 = bf16[128,8,128]{0,2,1:T(8,128)(2,1)S(1)} collective-permute-done((bf16[128,8,128]{0,2,1:T(8,128)(2,1)S(1)}, bf16[128,8,128]{0,2,1:T(8,128)(2,1)S(1)}, u32[]{:S(2)}, u32[]{:S(2)}) %collective-permute-start.11) | collective-permute-done | bytes 262176 | tf_op jit(solution)/shard_map/ppermute | solution.py:16
  85.4 6.3 %copy.211 = bf16[1,128,5376]{1,0,2:T(2,128)(2,1)S(1)} copy(bf16[1,128,5376]{2,1,0:T(8,128)(2,1)} %param.10) | data formatting | bytes 2752512 | tf_op args[0]
  92.2 30.3 %reduce = bf16[5376,128]{1,0:T(8,128)(2,1)} reduce(bf16[5376,1,128]{2,1,0:T(2,128)(2,1)S(1)} %bitcast.178, bf16[]{:T(256)} %broadcast.142), dimensions={1}, to_apply=%bitcast.157.reduce_sub_computation | reduce | bytes 2752514
  122.4 3.2 %reshape.256 = bf16[8,2,43008]{2,1,0:T(2,128)(2,1)S(1)} reshape(bf16[5376,128]{1,0:T(8,128)(2,1)} %reduce) | data formatting | bytes 2752512
  125.7 71.0 %all_to_all.36 = bf16[8,2,43008]{2,1,0:T(2,128)(2,1)} all-to-all(bf16[8,2,43008]{2,1,0:T(2,128)(2,1)S(1)} %reshape.256), channel_id=1, replica_groups=mesh['dp'=8,'ctx'=4] {'dp'}, dimensions={0} | all-to-all | bytes 2752512 | tf_op jit(solution)/shard_map/all_to_all | solution.py:50
  196.7 4.5 %reshape.257 = bf16[5376,1,128]{2,1,0:T(2,128)(2,1)S(1)} reshape(bf16[8,2,43008]{2,1,0:T(2,128)(2,1)} %all_to_all.36) | data formatting | bytes 2752512
  202.5 29.1 %all-gather.2.cloned.1.call-done = bf16[8,128,4096]{2,1,0:T(8,128)(2,1)} async-done(((bf16[1,128,4096]{2,1,0:T(8,128)(2,1)}), bf16[8,128,4096]{2,1,0:T(8,128)(2,1)}) %all-gather.2.cloned.1.call-update) | async-done | bytes 8388624 | tf_op jit(solution)/shard_map/all_gather | solution.py:120
  231.6 10.2 %bitcast_convert_fusion = bf16[4096,672]{0,1:T(8,128)(2,1)} fusion(bf16[8,128,672]{1,2,0:T(8,128)(2,1)} %bitcast.192, bf16[8,128,4096]{2,1,0:T(8,128)(2,1)} %all-gather.2.cloned.1.call-done), kind=kOutput, calls=%fused_computation | convolution fusion | flops 5639897088 | bytes 15269888 | tf_op jit(solution)/shard_map/btp,btd->pd/dot_general | solution.py:126
  241.8 11.1 %fusion.18 = bf16[8,128,672]{1,2,0:T(8,128)(2,1)} fusion(bf16[8,128,4096]{2,1,0:T(8,128)(2,1)} %all-gather.2.cloned.1.call-done, bf16[672,4096]{1,0:T(8,128)(2,1)} %param.19), kind=kOutput, calls=%fused_computation.20 | convolution fusion | flops 5637832704 | bytes 15269888 | tf_op jit(solution)/shard_map/btp,dp->btd/dot_general | solution.py:121
  252.9 3.6 %all-to-all-start = ((bf16[8,128,672]{1,2,0:T(8,128)(2,1)}), bf16[8,128,672]{1,2,0:T(8,128)(2,1)S(1)}, u32[]{:S(2)}, u32[]{:S(2)}) async-start(bf16[8,128,672]{1,2,0:T(8,128)(2,1)} %fusion.18), calls=%async_computation | async-start | bytes 2752512 | tf_op jit(solution)/shard_map/all_to_all | solution.py:122
  256.4 53.0 %all-reduce.4 = (f32[128]{0:T(128)}, f32[128]{0:T(128)}) all-reduce(f32[128]{0:T(128)S(1)} %get-tuple-element.28, f32[128]{0:T(128)S(1)} %get-tuple-element.30), channel_id=1, replica_groups=mesh['dp'=8,'ctx'=4] {'dp','ctx'}, use_global_device_ids=true, to_apply=%region_9.10 | all-reduce | flops 256 | bytes 2048 | tf_op jit(solution)/shard_map/psum | solution.py:117
  311.0 3.2 %convert_element_type.126 = f32[1024,672]{0,1:T(8,128)} convert(bf16[1024,672]{0,1:T(8,128)(2,1)} %reduce-scatter.2.cloned.1.call-done) | non-fusion elementwise | flops 688128 | bytes 4128768 | tf_op jit(solution)/shard_map/convert_element_type | solution.py:132
  (94 shorter events, 43.5 us)
Async XLA Ops:
  7.2 13.5 %copy-start.4 = (bf16[1,128,1024]{2,1,0:T(8,128)(2,1)S(1)}, bf16[1,128,1024]{2,1,0:T(8,128)(2,1)}, u32[]{:S(2)}) copy-start(bf16[1,128,1024]{2,1,0:T(8,128)(2,1)} %param.13) | copy-start | bytes 786436
  7.2 18.5 %copy-start.2 = (bf16[1,128,2048]{2,1,0:T(8,128)(2,1)S(1)}, bf16[1,128,2048]{2,1,0:T(8,128)(2,1)}, u32[]{:S(2)}) copy-start(bf16[1,128,2048]{2,1,0:T(8,128)(2,1)} %param.11) | copy-start | bytes 1572868
  7.2 224.4 %all-gather.2.cloned.1.call-start = ((), (), s32[]{:S(2)}) async-start(), calls=%async_computation.3 | async-start | bytes 9437184 | tf_op jit(solution)/shard_map/all_gather | solution.py:120
  8.6 17.0 %copy-start = (f32[128,8,128]{2,0,1:T(8,128)}, f32[128,8,128]{2,0,1:T(8,128)S(1)}, u32[]{:S(2)}) copy-start(f32[128,8,128]{2,0,1:T(8,128)S(1)} %copy.177) | copy-start | bytes 1572868
  10.5 15.9 %copy-start.5 = (f32[128]{0:T(128)S(1)}, f32[128]{0:T(128)}, u32[]{:S(2)}) copy-start(f32[128]{0:T(128)} %param.17) | copy-start | bytes 1540
  11.7 19.7 %collective-permute-start.2 = (bf16[128,8,128]{2,0,1:T(8,128)(2,1)}, bf16[128,8,128]{2,0,1:T(8,128)(2,1)}, u32[]{:S(2)}, u32[]{:S(2)}) collective-permute-start(bf16[128,8,128]{2,0,1:T(8,128)(2,1)} %pad_maximum_fusion.3), channel_id=1, source_target_pairs={{0,3},{4,7},{8,11},{12,15},{16,19},{20,23},{24,27},{28,31}} | collective-permute-start | bytes 786440 | tf_op jit(solution)/shard_map/ppermute | solution.py:16
  16.7 16.2 %collective-permute-start = (bf16[128,8,128]{2,0,1:T(8,128)(2,1)}, bf16[128,8,128]{2,0,1:T(8,128)(2,1)}, u32[]{:S(2)}, u32[]{:S(2)}) collective-permute-start(bf16[128,8,128]{2,0,1:T(8,128)(2,1)} %pad_maximum_fusion.3), channel_id=1, source_target_pairs={{0,1},{1,2},{2,3},{4,5},{5,6},{6,7},{8,9},{9,10},{10,11},{12,13},{... | collective-permute-start | bytes 786440 | tf_op jit(solution)/shard_map/ppermute | solution.py:16
  18.7 14.3 %collective-permute-start.1 = (bf16[128,8,128]{2,0,1:T(8,128)(2,1)}, bf16[128,8,128]{2,0,1:T(8,128)(2,1)}, u32[]{:S(2)}, u32[]{:S(2)}) collective-permute-start(bf16[128,8,128]{2,0,1:T(8,128)(2,1)} %pad_maximum_fusion.3), channel_id=1, source_target_pairs={{0,2},{1,3},{4,6},{5,7},{8,10},{9,11},{12,14},{13,15},{16,18},{17,... | collective-permute-start | bytes 786440 | tf_op jit(solution)/shard_map/ppermute | solution.py:16
  21.7 14.2 %collective-permute-start.3 = (bf16[128,8,128]{2,0,1:T(8,128)(2,1)}, bf16[128,8,128]{2,0,1:T(8,128)(2,1)}, u32[]{:S(2)}, u32[]{:S(2)}) collective-permute-start(bf16[128,8,128]{2,0,1:T(8,128)(2,1)} %copy.187), channel_id=1, source_target_pairs={{0,1},{1,2},{2,3},{4,5},{5,6},{6,7},{8,9},{9,10},{10,11},{12,13},{... | collective-permute-start | bytes 786440 | tf_op jit(solution)/shard_map/ppermute | solution.py:16
  23.6 12.3 %collective-permute-start.4 = (bf16[128,8,128]{2,0,1:T(8,128)(2,1)}, bf16[128,8,128]{2,0,1:T(8,128)(2,1)}, u32[]{:S(2)}, u32[]{:S(2)}) collective-permute-start(bf16[128,8,128]{2,0,1:T(8,128)(2,1)} %copy.187), channel_id=1, source_target_pairs={{0,2},{1,3},{4,6},{5,7},{8,10},{9,11},{12,14},{13,15},{16,18},{17,... | collective-permute-start | bytes 786440 | tf_op jit(solution)/shard_map/ppermute | solution.py:16
  26.8 4.5 %copy-start.7 = (s32[1,128]{1,0:T(1,128)S(1)}, s32[1,128]{1,0:T(1,128)}, u32[]{:S(2)}) copy-start(s32[1,128]{1,0:T(1,128)} %param.15) | copy-start | bytes 1540
  31.4 8.4 %collective-permute-start.5 = (bf16[128,8,128]{2,0,1:T(8,128)(2,1)}, bf16[128,8,128]{2,0,1:T(8,128)(2,1)S(1)}, u32[]{:S(2)}, u32[]{:S(2)}) collective-permute-start(bf16[128,8,128]{2,0,1:T(8,128)(2,1)} %copy.187), channel_id=1, source_target_pairs={{0,3},{4,7},{8,11},{12,15},{16,19},{20,23},{24,27},{28,31}} | collective-permute-start | bytes 786440 | tf_op jit(solution)/shard_map/ppermute | solution.py:16
  35.0 4.8 %copy-start.3 = (bf16[128,8,2,128,1]{0,3,2,4,1:T(8,128)(2,1)S(1)}, bf16[128,8,2,128,1]{0,3,2,4,1:T(8,128)(2,1)}, u32[]{:S(2)}) copy-start(bf16[128,8,2,128,1]{0,3,2,4,1:T(8,128)(2,1)} %copy.224) | copy-start | bytes 1572868
  54.2 13.7 %collective-permute-start.6 = (bf16[128,8,128]{2,0,1:T(8,128)(2,1)}, bf16[128,8,128]{2,0,1:T(8,128)(2,1)}, u32[]{:S(2)}, u32[]{:S(2)}) collective-permute-start(bf16[128,8,128]{2,0,1:T(8,128)(2,1)} %get-tuple-element.40), channel_id=1, source_target_pairs={{1,0},{2,1},{3,2},{5,4},{6,5},{7,6},{9,8},{10,9},{11,10},{13,12},{... | collective-permute-start | bytes 786440 | tf_op jit(solution)/shard_map/ppermute | solution.py:16
  55.5 13.8 %collective-permute-start.7 = (bf16[128,8,128]{2,0,1:T(8,128)(2,1)}, bf16[128,8,128]{2,0,1:T(8,128)(2,1)}, u32[]{:S(2)}, u32[]{:S(2)}) collective-permute-start(bf16[128,8,128]{2,0,1:T(8,128)(2,1)} %get-tuple-element.42), channel_id=1, source_target_pairs={{2,0},{3,1},{6,4},{7,5},{10,8},{11,9},{14,12},{15,13},{18,16},{19,... | collective-permute-start | bytes 786440 | tf_op jit(solution)/shard_map/ppermute | solution.py:16
  56.8 14.2 %collective-permute-start.8 = (bf16[128,8,128]{2,0,1:T(8,128)(2,1)}, bf16[128,8,128]{2,0,1:T(8,128)(2,1)}, u32[]{:S(2)}, u32[]{:S(2)}) collective-permute-start(bf16[128,8,128]{2,0,1:T(8,128)(2,1)} %get-tuple-element.41), channel_id=1, source_target_pairs={{3,0},{7,4},{11,8},{15,12},{19,16},{23,20},{27,24},{31,28}} | collective-permute-start | bytes 786440 | tf_op jit(solution)/shard_map/ppermute | solution.py:16
  62.7 9.9 %copy-start.1 = (f32[128,8,128]{2,0,1:T(8,128)S(1)}, f32[128,8,128]{2,0,1:T(8,128)}, u32[]{:S(2)}) copy-start(f32[128,8,128]{2,0,1:T(8,128)} %copy-done) | copy-start | bytes 1572868
  62.7 9.9 %copy-start.6 = (f32[128]{0:T(128)S(1)}, f32[128]{0:T(128)}, u32[]{:S(2)}) copy-start(f32[128]{0:T(128)} %param.18) | copy-start | bytes 1540
  65.2 11.1 %collective-permute-start.10 = (bf16[128,8,128]{0,2,1:T(8,128)(2,1)S(1)}, bf16[128,8,128]{0,2,1:T(8,128)(2,1)S(1)}, u32[]{:S(2)}, u32[]{:S(2)}) collective-permute-start(bf16[128,8,128]{0,2,1:T(8,128)(2,1)S(1)} %get-tuple-element.45), channel_id=1, source_target_pairs={{2,0},{3,1},{6,4},{7,5},{10,8},{11,9},{14,12},{15,13},{18,16},{19,... | collective-permute-start | bytes 786440 | tf_op jit(solution)/shard_map/ppermute | solution.py:16
  66.5 16.2 %collective-permute-start.11 = (bf16[128,8,128]{0,2,1:T(8,128)(2,1)S(1)}, bf16[128,8,128]{0,2,1:T(8,128)(2,1)S(1)}, u32[]{:S(2)}, u32[]{:S(2)}) collective-permute-start(bf16[128,8,128]{0,2,1:T(8,128)(2,1)S(1)} %get-tuple-element.44), channel_id=1, source_target_pairs={{3,0},{7,4},{11,8},{15,12},{19,16},{23,20},{27,24},{31,28}} | collective-permute-start | bytes 786440 | tf_op jit(solution)/shard_map/ppermute | solution.py:16
  67.8 14.9 %collective-permute-start.9 = (bf16[128,8,128]{0,2,1:T(8,128)(2,1)S(1)}, bf16[128,8,128]{0,2,1:T(8,128)(2,1)S(1)}, u32[]{:S(2)}, u32[]{:S(2)}) collective-permute-start(bf16[128,8,128]{0,2,1:T(8,128)(2,1)S(1)} %get-tuple-element.43), channel_id=1, source_target_pairs={{1,0},{2,1},{3,2},{5,4},{6,5},{7,6},{9,8},{10,9},{11,10},{13,12},{... | collective-permute-start | bytes 786440 | tf_op jit(solution)/shard_map/ppermute | solution.py:16
  85.1 225.9 %reduce-scatter.2.cloned.1.call-start = ((), (), s32[]{:S(2)}) async-start(), calls=%async_computation.4 | async-start | bytes 6881280 | tf_op jit(solution)/shard_map/reduce_scatter | solution.py:125
  252.9 56.6 %all-to-all-start = ((bf16[8,128,672]{1,2,0:T(8,128)(2,1)}), bf16[8,128,672]{1,2,0:T(8,128)(2,1)S(1)}, u32[]{:S(2)}, u32[]{:S(2)}) async-start(bf16[8,128,672]{1,2,0:T(8,128)(2,1)} %fusion.18), calls=%async_computation | async-start | bytes 2752512 | tf_op jit(solution)/shard_map/all_to_all | solution.py:122
Sparse Core Ops, SparseCore 0:
  85.2 146.3 all-gather.1
  241.9 51.8 reduce-scatter.1
where the time goes:
time: 322 us; the launch traced here: 321 us
  blocking collectives  124 us (39%)
  other arithmetic  49.7 us (15%)
  waiting for transfers between devices  43.6 us (14%)
  matrix products  32.5 us (10%)
  local copies, waits for them, and re-layouts  30 us (9%)
  starting transfers between devices  26 us (8%)
  between operations  15.2 us (5%)
    all_to_all x1, blocking collectives, shards(): lax.all_to_all(inputs, 'dp', split_axis=2, concat_axis=0, tiled=True)  71 us
    psum x1, blocking collectives, shards(): dq_gain_all, dk_gain_all = lax.psum((dq_gain, dk_gain), ('dp', 'ctx'))  53 us
    unnamed x2, other arithmetic  30.4 us
    all_gather x1, waiting for transfers between devices, shards(): gathered = lax.all_gather(d_proj, 'dp', axis=0, tiled=True)  29.1 us
    ppermute x12, starting transfers between devices, from_behind(): lax.ppermute(value, axis, [(source, source + steps) for source in range(i...  22.2 us
    unnamed x27, local copies, waits for them, and re-layouts  21.7 us
    ppermute x12, waiting for transfers between devices, from_behind(): lax.ppermute(value, axis, [(source, source + steps) for source in range(i...  14.4 us
    dot_general x1, matrix products, shards(): jnp.einsum('btp,dp->btd', gathered, weight, preferred_element_type=jnp.fl...  11.1 us
  transfers between devices with their start and end apart: 15, of which 6 were waited for; matrix products, arithmetic and copies ran while one was open for 24% of the time, Pallas kernels for 0%

commit v1 on v0

--- a/solution.py
+++ b/solution.py
@@ -3,6 +3,7 @@
 import jax.numpy as jnp
 from jax import lax
 from jax.sharding import PartitionSpec as P
+from jax.lax import axis_index, axis_size, ppermute
 
 REACH = 8
 score_scale = 168.0 ** (-0.5)
@@ -117,7 +118,16 @@
     dq_gain_all, dk_gain_all = lax.psum((dq_gain, dk_gain), ("dp", "ctx"))
     dv_proj = dv_total.reshape(tok_rows, key_heads * head_width)
     d_proj = jnp.concatenate([dq_proj, dk_proj, dv_proj], axis=-1).astype(jnp.bfloat16)[None]
-    gathered = lax.all_gather(d_proj, "dp", axis=0, tiled=True)
+    f_next = axis_index("dp")
+    w_next = axis_size("dp")
+    prior, kept_arr, earlier = (w_next, f_next, d_proj.shape[0])
+    r1, raw_out = (d_proj, 1)
+    while raw_out < prior:
+        block_next = tuple(((rr, (rr - raw_out) % prior) for rr in range(prior)))
+        fresh = ppermute(r1, "dp", block_next)
+        r1 = jnp.concatenate([r1, fresh], 0)
+        raw_out = 2 * raw_out
+    gathered = jnp.roll(r1, kept_arr * earlier, 0)
     d_cols = jnp.einsum("btp,dp->btd", gathered, weight, preferred_element_type=jnp.float32)
     d_inputs = lax.all_to_all(
         d_cols.astype(jnp.bfloat16), "dp", split_axis=0, concat_axis=2, tiled=True

time: 322 us -> 491 us (1.52)
  waiting for transfers between devices: 43.6 us -> 238 us
  blocking collectives: 124 us -> 55.1 us
  local copies, waits for them, and re-layouts: 30 us -> 50.2 us
  starting transfers between devices: 26 us -> 43.9 us
  other arithmetic: 49.7 us -> 55.2 us
    all_to_all x0 -> x1, waiting for transfers between devices: none -> 158 us  [shards(): lax.all_to_all(inputs, 'dp', split_axis=2, concat_axis=0, tiled=True)]
    all_to_all x1 -> x0, blocking collectives: 71 us -> none  [shards(): lax.all_to_all(inputs, 'dp', split_axis=2, concat_axis=0, tiled=True)]
    ppermute x0 -> x3, waiting for transfers between devices: none -> 66.5 us  [shards(): fresh = ppermute(r1, 'dp', block_next)]
    all_gather x1 -> x0, waiting for transfers between devices: 29.1 us -> none  [shards(): gathered = lax.all_gather(d_proj, 'dp', axis=0, tiled=True)]
    unnamed x27 -> x44, local copies, waits for them, and re-layouts: 21.7 us -> 35.2 us
    all_to_all x0 -> x1, starting transfers between devices: none -> 8.28 us  [shards(): lax.all_to_all(inputs, 'dp', split_axis=2, concat_axis=0, tiled=True)]
    ppermute x0 -> x3, starting transfers between devices: none -> 6.66 us  [shards(): fresh = ppermute(r1, 'dp', block_next)]
    unnamed x2 -> x3, other arithmetic: 30.4 us -> 32.5 us
  transfers between devices with their start and end apart: 15 -> 18, of which waited for: 6 -> 8; matrix products, arithmetic and copies ran while one was open for 24% -> 17% of each run, Pallas kernels for 0% -> 0%
where the time goes in v1:
time: 491 us; the launch traced here: 490 us
  waiting for transfers between devices  238 us (48%)
  other arithmetic  55.2 us (11%)
  blocking collectives  55.1 us (11%)
  local copies, waits for them, and re-layouts  50.2 us (10%)
  starting transfers between devices  43.9 us (9%)
  matrix products  32.5 us (7%)
  between operations  15.2 us (3%)
    all_to_all x1, waiting for transfers between devices, shards(): lax.all_to_all(inputs, 'dp', split_axis=2, concat_axis=0, tiled=True)  158 us
    ppermute x3, waiting for transfers between devices, shards(): fresh = ppermute(r1, 'dp', block_next)  66.5 us
    psum x1, blocking collectives, shards(): dq_gain_all, dk_gain_all = lax.psum((dq_gain, dk_gain), ('dp', 'ctx'))  55.1 us
    unnamed x44, local copies, waits for them, and re-layouts  35.2 us
    unnamed x3, other arithmetic  32.5 us
    ppermute x12, starting transfers between devices, from_behind(): lax.ppermute(value, axis, [(source, source + steps) for source in range(i...  22.2 us
    ppermute x12, waiting for transfers between devices, from_behind(): lax.ppermute(value, axis, [(source, source + steps) for source in range(i...  13.6 us
    dot_general x1, matrix products, shards(): jnp.einsum('btp,dp->btd', gathered, weight, preferred_element_type=jnp.fl...  10.8 us
  transfers between devices with their start and end apart: 18, of which 8 were waited for; matrix products, arithmetic and copies ran while one was open for 17% of the time, Pallas kernels for 0%

profile of v1, /device:TPU:0, one launch (start us, length us, event | category | flops | bytes accessed | tf_op | source)
XLA Modules:
  0.0 489.8 jit_solution(1606946103892107766)
XLA Ops:
  10.9 5.0 %collective-permute-start.2 = (bf16[128,8,128]{2,0,1:T(8,128)(2,1)S(1)}, bf16[128,8,128]{2,0,1:T(8,128)(2,1)}, u32[]{:S(2)}, u32[]{:S(2)}) collective-permute-start(bf16[128,8,128]{2,0,1:T(8,128)(2,1)S(1)} %pad_maximum_fusion.5), channel_id=1, source_target_pairs={{0,3},{4,7},{8,11},{12,15},{16,19},{20,23},{24,27},{28,31}} | collective-permute-start | bytes 786440 | tf_op jit(solution)/shard_map/ppermute | solution.py:17
  36.7 2.2 collective-permute-done.5
  38.9 2.4 fusion.7
  44.4 2.5 fusion.66
  46.8 3.0 fusion.65
  70.2 3.7 collective-permute-done.8
  78.0 6.3 %collective-permute-done.11 = bf16[128,8,128]{0,2,1:T(8,128)(2,1)S(1)} collective-permute-done((bf16[128,8,128]{0,2,1:T(8,128)(2,1)S(1)}, bf16[128,8,128]{0,2,1:T(8,128)(2,1)S(1)}, u32[]{:S(2)}, u32[]{:S(2)}) %collective-permute-start.11) | collective-permute-done | bytes 262176 | tf_op jit(solution)/shard_map/ppermute | solution.py:17
  86.7 4.5 collective-permute-start.12
  91.3 22.0 %collective-permute-done.12 = bf16[1,128,4096]{2,1,0:T(8,128)(2,1)S(1)} collective-permute-done((bf16[1,128,4096]{2,1,0:T(8,128)(2,1)S(1)}, bf16[1,128,4096]{2,1,0:T(8,128)(2,1)S(1)}, u32[]{:S(2)}, u32[]{:S(2)}) %collective-permute-start.12) | collective-permute-done | bytes 1048608 | tf_op jit(solution)/shard_map/ppermute | solution.py:127
  115.0 44.5 %collective-permute-done.13 = bf16[2,128,4096]{2,1,0:T(8,128)(2,1)S(1)} collective-permute-done((bf16[2,128,4096]{2,1,0:T(8,128)(2,1)S(1)}, bf16[2,128,4096]{2,1,0:T(8,128)(2,1)S(1)}, u32[]{:S(2)}, u32[]{:S(2)}) %collective-permute-start.13) | collective-permute-done | bytes 2097184 | tf_op jit(solution)/shard_map/ppermute | solution.py:127
  159.5 3.1 pad_maximum_fusion
  163.2 6.8 %copy.211 = bf16[1,128,5376]{1,0,2:T(2,128)(2,1)} copy(bf16[1,128,5376]{2,1,0:T(8,128)(2,1)} %param.10) | data formatting | bytes 2752512 | tf_op args[0]
  170.5 31.3 %reduce = bf16[5376,128]{1,0:T(8,128)(2,1)} reduce(bf16[5376,1,128]{2,1,0:T(2,128)(2,1)} %bitcast.176, bf16[]{:T(256)} %broadcast.143), dimensions={1}, to_apply=%bitcast.157.reduce_sub_computation | reduce | bytes 2752514
  201.8 4.1 reshape.256
  205.9 8.3 %all-to-all-start.1 = ((bf16[8,2,43008]{2,1,0:T(2,128)(2,1)}), bf16[8,2,43008]{2,1,0:T(2,128)(2,1)}, u32[]{:S(2)}, u32[]{:S(2)}) async-start(bf16[8,2,43008]{2,1,0:T(2,128)(2,1)} %reshape.256), calls=%async_computation.1 | async-start | bytes 2752512 | tf_op jit(solution)/shard_map/all_to_all | solution.py:51
  215.5 157.7 %all-to-all-done.1 = bf16[8,2,43008]{2,1,0:T(2,128)(2,1)} async-done(((bf16[8,2,43008]{2,1,0:T(2,128)(2,1)}), bf16[8,2,43008]{2,1,0:T(2,128)(2,1)}, u32[]{:S(2)}, u32[]{:S(2)}) %all-to-all-start.1) | async-done | bytes 1376288 | tf_op jit(solution)/shard_map/all_to_all | solution.py:51
  373.3 6.1 %reshape.257 = bf16[5376,1,128]{2,1,0:T(2,128)(2,1)} reshape(bf16[8,2,43008]{2,1,0:T(2,128)(2,1)} %all-to-all-done.1) | data formatting | bytes 2752512
  382.8 4.7 constant_dynamic-update-slice_fusion.4
  391.2 4.6 constant_dynamic-update-slice_fusion
  395.8 10.0 %bitcast_convert_fusion = bf16[4096,672]{0,1:T(8,128)(2,1)} fusion(bf16[8,128,672]{1,2,0:T(8,128)(2,1)S(1)} %bitcast.190, bf16[16,128,4096]{2,1,0:T(8,128)(2,1)} %constant_dynamic-update-slice_fusion, s32[]{:T(128)S(6)} %select_n.19), kind=kOutput, calls=%fused_computation | convolution fusion | flops 5639897088 | bytes 15269892 | tf_op jit(solution)/shard_map/btp,btd->pd/dot_general | solution.py:136
  405.9 10.8 %fusion.23 = bf16[8,128,672]{1,2,0:T(8,128)(2,1)} fusion(bf16[672,4096]{1,0:T(8,128)(2,1)} %param.19, bf16[16,128,4096]{2,1,0:T(8,128)(2,1)} %constant_dynamic-update-slice_fusion, s32[]{:T(128)S(6)} %select_n.19), kind=kOutput, calls=%fused_computation.25 | convolution fusion | flops 5637832704 | bytes 15269892 | tf_op jit(solution)/shard_map/btp,dp->btd/dot_general | solution.py:131
  416.7 6.5 %all-to-all-start = ((bf16[8,128,672]{1,2,0:T(8,128)(2,1)}), bf16[8,128,672]{1,2,0:T(8,128)(2,1)S(1)}, u32[]{:S(2)}, u32[]{:S(2)}) async-start(bf16[8,128,672]{1,2,0:T(8,128)(2,1)} %fusion.23), calls=%async_computation | async-start | bytes 2752512 | tf_op jit(solution)/shard_map/all_to_all | solution.py:132
  423.1 55.1 %all-reduce.4 = (f32[128]{0:T(128)}, f32[128]{0:T(128)}) all-reduce(f32[128]{0:T(128)S(1)} %get-tuple-element.28, f32[128]{0:T(128)S(1)} %get-tuple-element.30), channel_id=1, replica_groups=mesh['dp'=8,'ctx'=4] {'dp','ctx'}, use_global_device_ids=true, to_apply=%region_9.10 | all-reduce | flops 256 | bytes 2048 | tf_op jit(solution)/shard_map/psum | solution.py:118
  479.7 3.2 convert_element_type.126
  (119 shorter events, 66.1 us)
Async XLA Ops:
  7.2 12.8 %copy-start.9 = (bf16[1,128,1024]{2,1,0:T(8,128)(2,1)S(1)}, bf16[1,128,1024]{2,1,0:T(8,128)(2,1)}, u32[]{:S(2)}) copy-start(bf16[1,128,1024]{2,1,0:T(8,128)(2,1)} %param.13) | copy-start | bytes 786436
  7.2 17.8 %copy-start.6 = (bf16[1,128,2048]{2,1,0:T(8,128)(2,1)S(1)}, bf16[1,128,2048]{2,1,0:T(8,128)(2,1)}, u32[]{:S(2)}) copy-start(bf16[1,128,2048]{2,1,0:T(8,128)(2,1)} %param.11) | copy-start | bytes 1572868
  8.6 16.4 %copy-start.2 = (f32[128,8,128]{2,0,1:T(8,128)}, f32[128,8,128]{2,0,1:T(8,128)S(1)}, u32[]{:S(2)}) copy-start(f32[128,8,128]{2,0,1:T(8,128)S(1)} %copy.177) | copy-start | bytes 1572868
  10.5 15.3 %copy-start.11 = (f32[128]{0:T(128)S(1)}, f32[128]{0:T(128)}, u32[]{:S(2)}) copy-start(f32[128]{0:T(128)} %param.17) | copy-start | bytes 1540
  10.9 21.2 %collective-permute-start.2 = (bf16[128,8,128]{2,0,1:T(8,128)(2,1)S(1)}, bf16[128,8,128]{2,0,1:T(8,128)(2,1)}, u32[]{:S(2)}, u32[]{:S(2)}) collective-permute-start(bf16[128,8,128]{2,0,1:T(8,128)(2,1)S(1)} %pad_maximum_fusion.5), channel_id=1, source_target_pairs={{0,3},{4,7},{8,11},{12,15},{16,19},{20,23},{24,27},{28,31}} | collective-permute-start | bytes 786440 | tf_op jit(solution)/shard_map/ppermute | solution.py:17
  15.9 17.6 %collective-permute-start = (bf16[128,8,128]{2,0,1:T(8,128)(2,1)S(1)}, bf16[128,8,128]{2,0,1:T(8,128)(2,1)}, u32[]{:S(2)}, u32[]{:S(2)}) collective-permute-start(bf16[128,8,128]{2,0,1:T(8,128)(2,1)S(1)} %pad_maximum_fusion.5), channel_id=1, source_target_pairs={{0,1},{1,2},{2,3},{4,5},{5,6},{6,7},{8,9},{9,10},{10,11},{12,13},{... | collective-permute-start | bytes 786440 | tf_op jit(solution)/shard_map/ppermute | solution.py:17
  17.9 15.7 %collective-permute-start.1 = (bf16[128,8,128]{2,0,1:T(8,128)(2,1)S(1)}, bf16[128,8,128]{2,0,1:T(8,128)(2,1)}, u32[]{:S(2)}, u32[]{:S(2)}) collective-permute-start(bf16[128,8,128]{2,0,1:T(8,128)(2,1)S(1)} %pad_maximum_fusion.5), channel_id=1, source_target_pairs={{0,2},{1,3},{4,6},{5,7},{8,10},{9,11},{12,14},{13,15},{16,18},{17,... | collective-permute-start | bytes 786440 | tf_op jit(solution)/shard_map/ppermute | solution.py:17
  21.0 15.7 %collective-permute-start.3 = (bf16[128,8,128]{2,0,1:T(8,128)(2,1)}, bf16[128,8,128]{2,0,1:T(8,128)(2,1)}, u32[]{:S(2)}, u32[]{:S(2)}) collective-permute-start(bf16[128,8,128]{2,0,1:T(8,128)(2,1)} %copy.187), channel_id=1, source_target_pairs={{0,1},{1,2},{2,3},{4,5},{5,6},{6,7},{8,9},{9,10},{10,11},{12,13},{... | collective-permute-start | bytes 786440 | tf_op jit(solution)/shard_map/ppermute | solution.py:17
  23.0 13.7 %collective-permute-start.4 = (bf16[128,8,128]{2,0,1:T(8,128)(2,1)}, bf16[128,8,128]{2,0,1:T(8,128)(2,1)}, u32[]{:S(2)}, u32[]{:S(2)}) collective-permute-start(bf16[128,8,128]{2,0,1:T(8,128)(2,1)} %copy.187), channel_id=1, source_target_pairs={{0,2},{1,3},{4,6},{5,7},{8,10},{9,11},{12,14},{13,15},{16,18},{17,... | collective-permute-start | bytes 786440 | tf_op jit(solution)/shard_map/ppermute | solution.py:17
  32.1 6.8 %collective-permute-start.5 = (bf16[128,8,128]{2,0,1:T(8,128)(2,1)}, bf16[128,8,128]{2,0,1:T(8,128)(2,1)S(1)}, u32[]{:S(2)}, u32[]{:S(2)}) collective-permute-start(bf16[128,8,128]{2,0,1:T(8,128)(2,1)} %copy.187), channel_id=1, source_target_pairs={{0,3},{4,7},{8,11},{12,15},{16,19},{20,23},{24,27},{28,31}} | collective-permute-start | bytes 786440 | tf_op jit(solution)/shard_map/ppermute | solution.py:17
  57.7 11.0 %collective-permute-start.6 = (bf16[128,8,128]{2,0,1:T(8,128)(2,1)}, bf16[128,8,128]{2,0,1:T(8,128)(2,1)}, u32[]{:S(2)}, u32[]{:S(2)}) collective-permute-start(bf16[128,8,128]{2,0,1:T(8,128)(2,1)} %get-tuple-element.42), channel_id=1, source_target_pairs={{1,0},{2,1},{3,2},{5,4},{6,5},{7,6},{9,8},{10,9},{11,10},{13,12},{... | collective-permute-start | bytes 786440 | tf_op jit(solution)/shard_map/ppermute | solution.py:17
  58.9 11.2 %collective-permute-start.7 = (bf16[128,8,128]{2,0,1:T(8,128)(2,1)}, bf16[128,8,128]{2,0,1:T(8,128)(2,1)}, u32[]{:S(2)}, u32[]{:S(2)}) collective-permute-start(bf16[128,8,128]{2,0,1:T(8,128)(2,1)} %get-tuple-element.44), channel_id=1, source_target_pairs={{2,0},{3,1},{6,4},{7,5},{10,8},{11,9},{14,12},{15,13},{18,16},{19,... | collective-permute-start | bytes 786440 | tf_op jit(solution)/shard_map/ppermute | solution.py:17
  60.2 13.6 %collective-permute-start.8 = (bf16[128,8,128]{2,0,1:T(8,128)(2,1)}, bf16[128,8,128]{2,0,1:T(8,128)(2,1)}, u32[]{:S(2)}, u32[]{:S(2)}) collective-permute-start(bf16[128,8,128]{2,0,1:T(8,128)(2,1)} %get-tuple-element.43), channel_id=1, source_target_pairs={{3,0},{7,4},{11,8},{15,12},{19,16},{23,20},{27,24},{31,28}} | collective-permute-start | bytes 786440 | tf_op jit(solution)/shard_map/ppermute | solution.py:17
  64.7 48.6 %copy-start = (bf16[1,128,2048]{2,1,0:T(8,128)(2,1)}, bf16[1,128,2048]{2,1,0:T(8,128)(2,1)S(1)}, u32[]{:S(2)}) copy-start(bf16[1,128,2048]{2,1,0:T(8,128)(2,1)S(1)} %concatenate.65) | copy-start | bytes 1572868
  66.0 11.9 %collective-permute-start.10 = (bf16[128,8,128]{0,2,1:T(8,128)(2,1)S(1)}, bf16[128,8,128]{0,2,1:T(8,128)(2,1)S(1)}, u32[]{:S(2)}, u32[]{:S(2)}) collective-permute-start(bf16[128,8,128]{0,2,1:T(8,128)(2,1)S(1)} %get-tuple-element.47), channel_id=1, source_target_pairs={{2,0},{3,1},{6,4},{7,5},{10,8},{11,9},{14,12},{15,13},{18,16},{19,... | collective-permute-start | bytes 786440 | tf_op jit(solution)/shard_map/ppermute | solution.py:17
  67.3 17.0 %collective-permute-start.11 = (bf16[128,8,128]{0,2,1:T(8,128)(2,1)S(1)}, bf16[128,8,128]{0,2,1:T(8,128)(2,1)S(1)}, u32[]{:S(2)}, u32[]{:S(2)}) collective-permute-start(bf16[128,8,128]{0,2,1:T(8,128)(2,1)S(1)} %get-tuple-element.46), channel_id=1, source_target_pairs={{3,0},{7,4},{11,8},{15,12},{19,16},{23,20},{27,24},{31,28}} | collective-permute-start | bytes 786440 | tf_op jit(solution)/shard_map/ppermute | solution.py:17
  68.6 15.6 %collective-permute-start.9 = (bf16[128,8,128]{0,2,1:T(8,128)(2,1)S(1)}, bf16[128,8,128]{0,2,1:T(8,128)(2,1)S(1)}, u32[]{:S(2)}, u32[]{:S(2)}) collective-permute-start(bf16[128,8,128]{0,2,1:T(8,128)(2,1)S(1)} %get-tuple-element.45), channel_id=1, source_target_pairs={{1,0},{2,1},{3,2},{5,4},{6,5},{7,6},{9,8},{10,9},{11,10},{13,12},{... | collective-permute-start | bytes 786440 | tf_op jit(solution)/shard_map/ppermute | solution.py:17
  85.6 27.7 %copy-start.4 = (bf16[1,128,1024]{2,1,0:T(8,128)(2,1)}, bf16[1,128,1024]{2,1,0:T(8,128)(2,1)S(1)}, u32[]{:S(2)}) copy-start(bf16[1,128,1024]{2,1,0:T(8,128)(2,1)S(1)} %copy.210) | copy-start | bytes 786436
  86.7 26.5 %collective-permute-start.12 = (bf16[1,128,4096]{2,1,0:T(8,128)(2,1)S(1)}, bf16[1,128,4096]{2,1,0:T(8,128)(2,1)S(1)}, u32[]{:S(2)}, u32[]{:S(2)}) collective-permute-start(bf16[1,128,4096]{2,1,0:T(8,128)(2,1)S(1)} %get-tuple-element.38), channel_id=1, source_target_pairs={{0,28},{4,0},{8,4},{12,8},{16,12},{20,16},{24,20},{28,24},{1,29},{... | collective-permute-start | bytes 3145736 | tf_op jit(solution)/shard_map/ppermute | solution.py:127
  113.4 46.1 %collective-permute-start.13 = (bf16[2,128,4096]{2,1,0:T(8,128)(2,1)S(1)}, bf16[2,128,4096]{2,1,0:T(8,128)(2,1)S(1)}, u32[]{:S(2)}, u32[]{:S(2)}) collective-permute-start(bf16[2,128,4096]{2,1,0:T(8,128)(2,1)S(1)} %pad_maximum_fusion.1), channel_id=1, source_target_pairs={{0,24},{4,28},{8,0},{12,4},{16,8},{20,12},{24,16},{28,20},{1,25},{... | collective-permute-start | bytes 6291464 | tf_op jit(solution)/shard_map/ppermute | solution.py:127
  162.6 220.2 %collective-permute-start.14 = (bf16[4,128,4096]{2,1,0:T(8,128)(2,1)}, bf16[4,128,4096]{2,1,0:T(8,128)(2,1)}, u32[]{:S(2)}, u32[]{:S(2)}) collective-permute-start(bf16[4,128,4096]{2,1,0:T(8,128)(2,1)} %pad_maximum_fusion), channel_id=1, source_target_pairs={{0,16},{4,20},{8,24},{12,28},{16,0},{20,4},{24,8},{28,12},{1,17},{... | collective-permute-start | bytes 12582920 | tf_op jit(solution)/shard_map/ppermute | solution.py:127
  205.9 167.4 %all-to-all-start.1 = ((bf16[8,2,43008]{2,1,0:T(2,128)(2,1)}), bf16[8,2,43008]{2,1,0:T(2,128)(2,1)}, u32[]{:S(2)}, u32[]{:S(2)}) async-start(bf16[8,2,43008]{2,1,0:T(2,128)(2,1)} %reshape.256), calls=%async_computation.1 | async-start | bytes 2752512 | tf_op jit(solution)/shard_map/all_to_all | solution.py:51
  214.2 265.5 %reduce-scatter.2.cloned.1.call-start = ((), (), s32[]{:S(2)}) async-start(), calls=%async_computation.3 | async-start | bytes 6881280 | tf_op jit(solution)/shard_map/reduce_scatter | solution.py:135
  416.7 61.5 %all-to-all-start = ((bf16[8,128,672]{1,2,0:T(8,128)(2,1)}), bf16[8,128,672]{1,2,0:T(8,128)(2,1)S(1)}, u32[]{:S(2)}, u32[]{:S(2)}) async-start(bf16[8,128,672]{1,2,0:T(8,128)(2,1)} %fusion.23), calls=%async_computation | async-start | bytes 2752512 | tf_op jit(solution)/shard_map/all_to_all | solution.py:132
  (8 other events, 47.3 us)
Sparse Core Ops, SparseCore 0:
  406.0 57.5 reduce-scatter.1
